TPU v7x, 512 devices: a whole 4x8x8 slice. The times are simulated.
512 devices in a mesh: dp: 32 (over x, z), tp: 16 (over y, core).
Axes of the slice: x: 4, y: 8, z: 8, core: 2. Of those that a mesh axis runs over, the one named last changes fastest.
Arguments:
- queries: bfloat16 [1024, 128, 576], P(('dp', 'tp')), may hold values from -40 to 40
- latent_cache: bfloat16 [1024, 256, 576], P(('dp', 'tp')), may hold values from -5 to 5
- lengths: int32 [1024], P(('dp', 'tp')), may hold values from 1 to 256, 65536 in all
- value_weight: bfloat16 [128, 512, 128], P('tp'), may hold values from -0.25 to 0.25
- output_weight: bfloat16 [16384, 7168], P('tp', 'dp'), may hold values from -0.046875 to 0.046875
Outputs:
- attended: bfloat16 [1024, 7168], P(('dp', 'tp'))
All inputs are finite; a program needn't handle non-finite values. No bound on the sum of `lengths` on one device may be relied on, other than what follows from the above.
Results may differ from a plain program's by a relative error of at most 0.0065.
Values may be sent and summed in bfloat16 or wider, within the bound.
No kernel may reach another device: no remote copies, remote signals or barrier semaphores. Data moves between devices by JAX's collectives and lax.ppermute only.
A program may use at most 64 MiB of HBM per device.

v0:
```python
import jax
import jax.numpy as jnp
from jax import lax
from jax.sharding import PartitionSpec as P

score_scale = 192.0 ** (-0.5)


def local(queries, latent_cache, lengths, value_weight, output_weight):
    requests = queries.shape[0]
    groups = lax.axis_size("tp")
    columns = lax.axis_size("dp")
    latent_width = value_weight.shape[1]
    scores = (
        jnp.einsum("rhe,rje->rhj", queries, latent_cache, preferred_element_type=jnp.float32)
        * score_scale
    )
    alive_mask = lax.broadcasted_iota(jnp.int32, scores.shape, 2) < lengths[:, None, None]
    scores = jnp.where(alive_mask, scores, -1e30)
    row_max = jnp.max(scores, axis=2, keepdims=True)
    powers = jnp.exp(scores - row_max)
    weights = (powers / jnp.sum(powers, axis=2, keepdims=True)).astype(jnp.bfloat16)
    mixture = jnp.einsum("rhj,rje->rhe", weights, latent_cache, preferred_element_type=jnp.float32)
    latent = mixture[:, :, :latent_width].astype(jnp.bfloat16)
    swapped = lax.all_to_all(latent, "tp", split_axis=1, concat_axis=0, tiled=True)
    local_heads = swapped.shape[1]
    stacked = swapped.reshape(groups, requests, local_heads, latent_width)
    everyone = lax.all_gather(stacked, "dp", axis=1, tiled=True)
    values = jnp.einsum(
        "gqhd,hde->gqhe", everyone, value_weight, preferred_element_type=jnp.float32
    )
    values = values.astype(jnp.bfloat16)
    all_values = values.reshape(groups * columns * requests, -1)
    summed = lax.psum_scatter(
        jnp.dot(all_values, output_weight, preferred_element_type=jnp.float32),
        "tp",
        scatter_dimension=0,
        tiled=True,
    )
    rounded = summed.astype(jnp.bfloat16)
    return lax.all_to_all(rounded, "dp", split_axis=0, concat_axis=1, tiled=True)


def solution(mesh):
    return jax.shard_map(
        local,
        mesh=mesh,
        in_specs=(
            P(("dp", "tp"), None, None),
            P(("dp", "tp"), None, None),
            P(("dp", "tp")),
            P("tp", None, None),
            P("tp", "dp"),
        ),
        out_specs=P(("dp", "tp"), None),
        check_vma=False,
    )
```

profile of v0, /device:TPU:2, one launch (start us, length us, event | category | flops | bytes accessed | tf_op | source)
XLA Modules:
  0.0 230.4 jit_solution(6659828259434857418)
XLA Ops:
  6.5 0.0 copy-start
  6.5 0.0 all-gather.2.cloned.1.call-start
  6.5 1.5 fusion.10
  8.1 0.2 fusion.15
  8.3 1.6 fusion.12
  9.9 0.3 copy.11
  10.2 18.2 %all_to_all.34 = bf16[2,128,512]{2,0,1:T(2,128)(2,1)S(1)} all-to-all(bf16[2,128,512]{2,0,1:T(2,128)(2,1)S(1)} %copy.11), channel_id=1, replica_groups=mesh['dp'=32,'tp'=16] {'tp'}, dimensions={1} | all-to-all | bytes 524288 | tf_op jit(solution)/shard_map/all_to_all | solution.py:25
  28.4 0.7 copy.27
  29.1 0.0 all-gather.2.cloned.1.call-update
  29.1 0.0 reduce-scatter.2.cloned.1.call-start
  29.2 104.3 %all-gather.2.cloned.1.call-done = bf16[16,64,8,512]{3,2,0,1:T(8,128)(2,1)} async-done(((bf16[16,2,8,512]{3,2,0,1:T(8,128)(2,1)}), bf16[16,64,8,512]{3,2,0,1:T(8,128)(2,1)}) %all-gather.2.cloned.1.call-update) | async-done | bytes 8388624 | tf_op jit(solution)/shard_map/all_gather | solution.py:28
  133.4 0.0 copy-done
  133.5 8.2 %convert_bitcast_fusion = bf16[16,64,8,128]{3,1,0,2:T(8,128)(2,1)S(1)} fusion(bf16[16,64,8,512]{3,2,0,1:T(8,128)(2,1)} %all-gather.2.cloned.1.call-done, bf16[8,512,128]{2,1,0:T(8,128)(2,1)S(1)} %copy-done), kind=kOutput, calls=%fused_computation.6 | convolution fusion | flops 1074790400 | bytes 11534336 | tf_op jit(solution)/shard_map/gqhd,hde->gqhe/dot_general | solution.py:29
  141.7 0.0 copy-start.1
  141.7 1.8 copy.14
  143.5 0.0 copy-done.1
  143.5 1.7 fusion.3
  145.2 0.0 reduce-scatter.2.cloned.1.call-update
  145.2 57.7 %reduce-scatter.2.cloned.1.call-done = f32[64,224]{1,0:T(8,128)} async-done(((f32[1024,224]{1,0:T(8,128)}), f32[64,224]{1,0:T(8,128)}) %reduce-scatter.2.cloned.1.call-update) | async-done | bytes 57360 | tf_op jit(solution)/shard_map/reduce_scatter | solution.py:34
  202.9 0.8 convert_element_type.16
  203.8 19.0 %all_to_all.35 = bf16[32,2,224]{2,1,0:T(2,128)(2,1)S(1)} all-to-all(bf16[32,2,224]{2,1,0:T(2,128)(2,1)S(1)} %all_to_all.28), channel_id=1, replica_groups=mesh['dp'=32,'tp'=16] {'dp'}, dimensions={0} | all-to-all | bytes 57344 | tf_op jit(solution)/shard_map/all_to_all | solution.py:41
  222.8 0.7 all_to_all.31
  (3 shorter events, 0.1 us)
Async XLA Ops:
  6.5 126.9 %copy-start = (bf16[8,512,128]{2,1,0:T(8,128)(2,1)S(1)}, bf16[8,512,128]{2,1,0:T(8,128)(2,1)}, u32[]{:S(2)}) copy-start(bf16[8,512,128]{2,1,0:T(8,128)(2,1)} %param.8) | copy-start | bytes 3145732
  6.5 126.9 %all-gather.2.cloned.1.call-start = ((), (), s32[]{:S(2)}) async-start(), calls=%async_computation.3 | async-start | bytes 8650752 | tf_op jit(solution)/shard_map/all_gather | solution.py:28
  29.1 173.8 %reduce-scatter.2.cloned.1.call-start = ((), (), s32[]{:S(2)}) async-start(), calls=%async_computation.4 | async-start | bytes 1114112 | tf_op jit(solution)/shard_map/reduce_scatter | solution.py:34
  141.7 1.8 copy-start.1
Sparse Core Ops, SparseCore 0:
  29.3 104.1 all-gather.1
  145.3 57.5 reduce-scatter.1
where the time goes:
time: 231 us; the launch traced here: 230 us
  waiting for transfers between devices  162 us (70%)
  blocking collectives  37.2 us (16%)
  between operations  13.5 us (6%)
  matrix products  13.1 us (6%)
  local copies, waits for them, and re-layouts  3.58 us (2%)
    all_gather x1, waiting for transfers between devices, local(): everyone = lax.all_gather(stacked, 'dp', axis=1, tiled=True)  104 us
    reduce_scatter x1, waiting for transfers between devices, local(): lax.psum_scatter(jnp.dot(all_values, output_weight, preferred_element_typ...  57.7 us
    all_to_all x1, blocking collectives, local(): lax.all_to_all(rounded, 'dp', split_axis=0, concat_axis=1, tiled=True)  19 us
    all_to_all x1, blocking collectives, local(): lax.all_to_all(latent, 'tp', split_axis=1, concat_axis=0, tiled=True)  18.2 us
    dot_general x1, matrix products, local(): jnp.einsum('gqhd,hde->gqhe', everyone, value_weight, preferred_element_ty...  8.21 us
  transfers between devices with their start and end apart: 2, of which 2 were waited for; matrix products, arithmetic and copies ran while one was open for 0% of the time, Pallas kernels for 0%

commit v1 on v0

--- a/solution.py
+++ b/solution.py
@@ -25,7 +25,9 @@
     swapped = lax.all_to_all(latent, "tp", split_axis=1, concat_axis=0, tiled=True)
     local_heads = swapped.shape[1]
     stacked = swapped.reshape(groups, requests, local_heads, latent_width)
-    everyone = lax.all_gather(stacked, "dp", axis=1, tiled=True)
+    everyone = jnp.concatenate(
+        lax.all_to_all(jnp.stack([stacked] * lax.axis_size("dp")), "dp", 0, 0), axis=1
+    )
     values = jnp.einsum(
         "gqhd,hde->gqhe", everyone, value_weight, preferred_element_type=jnp.float32
     )

time: 231 us -> 345 us (1.49)
  blocking collectives: 37.2 us -> 234 us
  waiting for transfers between devices: 162 us -> 54.4 us
  local copies, waits for them, and re-layouts: 3.58 us -> 30.9 us
    all_to_all x0 -> x1, blocking collectives: none -> 198 us  [local(): lax.all_to_all(jnp.stack([stacked] * lax.axis_size('dp')), 'dp', 0, 0)]
    all_gather x1 -> x0, waiting for transfers between devices: 104 us -> none  [local(): everyone = lax.all_gather(stacked, 'dp', axis=1, tiled=True)]
    reshape x0 -> x2, local copies, waits for them, and re-layouts: none -> 20 us  [local(): jnp.concatenate(lax.all_to_all(jnp.stack([stacked] * lax.axis_size('dp'))...]
    another operation x0 -> x1, local copies, waits for them, and re-layouts: none -> 7.81 us  [local(): jnp.stack([stacked] * lax.axis_size('dp'))]
  transfers between devices with their start and end apart: 2 -> 1, of which waited for: 2 -> 1; matrix products, arithmetic and copies ran while one was open for 0% -> 0% of each run, Pallas kernels for 0% -> 0%
where the time goes in v1:
time: 345 us
  blocking collectives  234 us (68%)
  waiting for transfers between devices  54.4 us (16%)
  local copies, waits for them, and re-layouts  30.9 us (9%)
  between operations  13.5 us (4%)
  matrix products  10.6 us (3%)
    all_to_all x1, blocking collectives, local(): lax.all_to_all(jnp.stack([stacked] * lax.axis_size('dp')), 'dp', 0, 0)  198 us
    reduce_scatter x1, waiting for transfers between devices, local(): lax.psum_scatter(jnp.dot(all_values, output_weight, preferred_element_typ...  54.4 us
    reshape x2, local copies, waits for them, and re-layouts, local(): jnp.concatenate(lax.all_to_all(jnp.stack([stacked] * lax.axis_size('dp'))...  20 us
    all_to_all x1, blocking collectives, local(): lax.all_to_all(rounded, 'dp', split_axis=0, concat_axis=1, tiled=True)  18.8 us
    all_to_all x1, blocking collectives, local(): lax.all_to_all(latent, 'tp', split_axis=1, concat_axis=0, tiled=True)  18.2 us
    another operation x1, local copies, waits for them, and re-layouts, local(): jnp.stack([stacked] * lax.axis_size('dp'))  7.81 us
  transfers between devices with their start and end apart: 1, of which 1 were waited for; matrix products, arithmetic and copies ran while one was open for 0% of the time, Pallas kernels for 0%

profile of v1, /device:TPU:2, one launch (start us, length us, event | category | flops | bytes accessed | tf_op | source)
XLA Modules:
  0.0 344.8 jit_solution(10724854811973056072)
XLA Ops:
  6.5 0.0 copy-start
  6.5 0.0 reduce-scatter.2.cloned.1.call-start
  6.5 1.5 fusion.6
  8.1 0.2 fusion.11
  8.3 1.6 fusion.8
  9.9 0.3 copy.11
  10.2 18.2 %all_to_all.39 = bf16[2,128,512]{2,0,1:T(2,128)(2,1)S(1)} all-to-all(bf16[2,128,512]{2,0,1:T(2,128)(2,1)S(1)} %copy.11), channel_id=1, replica_groups=mesh['dp'=32,'tp'=16] {'tp'}, dimensions={1} | all-to-all | bytes 524288 | tf_op jit(solution)/shard_map/all_to_all | solution.py:25
  28.4 0.2 copy.12
  28.6 7.8 %stack.3 = bf16[32,16,2,8,512]{4,2,1,3,0:T(2,128)(2,1)S(1)} broadcast(bf16[16,2,8,512]{3,1,0,2:T(2,128)(2,1)S(1)} %copy.12), dimensions={1,2,3,4} | broadcast | bytes 8650752 | tf_op jit(solution)/shard_map/stack | solution.py:29
  36.4 197.5 %all_to_all.40 = bf16[32,16,2,8,512]{4,2,1,3,0:T(2,128)(2,1)S(1)} all-to-all(bf16[32,16,2,8,512]{4,2,1,3,0:T(2,128)(2,1)S(1)} %stack.3), channel_id=1, replica_groups=mesh['dp'=32,'tp'=16] {'dp'}, dimensions={0} | all-to-all | bytes 16777216 | tf_op jit(solution)/shard_map/all_to_all | solution.py:29
  233.9 7.0 %copy.13 = bf16[16,32,2,8,512]{4,2,1,0,3:T(2,128)(2,1)} copy(bf16[16,32,2,8,512]{4,2,0,3,1:T(2,128)(2,1)S(1)} %bitcast.26) | data formatting | bytes 16777216 | tf_op jit(solution)/shard_map/reshape | solution.py:28
  240.9 13.1 %reshape.19 = bf16[16,64,8,512]{3,1,0,2:T(8,128)(2,1)} reshape(bf16[16,32,2,8,512]{4,2,1,0,3:T(2,128)(2,1)} %copy.13) | data formatting | bytes 16777216 | tf_op jit(solution)/shard_map/reshape | solution.py:28
  254.0 0.0 copy-done
  254.0 5.7 %convert_bitcast_fusion = bf16[16,64,8,128]{3,1,0,2:T(8,128)(2,1)S(1)} fusion(bf16[16,64,8,512]{3,1,0,2:T(8,128)(2,1)} %reshape.19, bf16[8,512,128]{2,1,0:T(8,128)(2,1)S(1)} %copy-done), kind=kOutput, calls=%fused_computation.4 | convolution fusion | flops 1074790400 | bytes 11534336 | tf_op jit(solution)/shard_map/gqhd,hde->gqhe/dot_general | solution.py:31
  259.7 0.0 copy-start.1
  259.7 1.8 copy.14
  261.5 0.0 copy-done.1
  261.5 1.7 fusion.1
  263.2 0.0 reduce-scatter.2.cloned.1.call-update
  263.2 54.4 %reduce-scatter.2.cloned.1.call-done = f32[64,224]{1,0:T(8,128)} async-done(((f32[1024,224]{1,0:T(8,128)}), f32[64,224]{1,0:T(8,128)}) %reduce-scatter.2.cloned.1.call-update) | async-done | bytes 57360 | tf_op jit(solution)/shard_map/reduce_scatter | solution.py:36
  317.6 0.8 convert_element_type.16
  318.5 18.8 %all_to_all.41 = bf16[32,2,224]{2,1,0:T(2,128)(2,1)S(1)} all-to-all(bf16[32,2,224]{2,1,0:T(2,128)(2,1)S(1)} %all_to_all.32), channel_id=1, replica_groups=mesh['dp'=32,'tp'=16] {'dp'}, dimensions={0} | all-to-all | bytes 57344 | tf_op jit(solution)/shard_map/all_to_all | solution.py:43
  337.3 0.7 all_to_all.35
  (3 shorter events, 0.1 us)
Async XLA Ops:
  6.5 247.4 %copy-start = (bf16[8,512,128]{2,1,0:T(8,128)(2,1)S(1)}, bf16[8,512,128]{2,1,0:T(8,128)(2,1)}, u32[]{:S(2)}) copy-start(bf16[8,512,128]{2,1,0:T(8,128)(2,1)} %param.8) | copy-start | bytes 3145732
  6.5 311.1 %reduce-scatter.2.cloned.1.call-start = ((), (), s32[]{:S(2)}) async-start(), calls=%async_computation.4 | async-start | bytes 1114112 | tf_op jit(solution)/shard_map/reduce_scatter | solution.py:36
  259.7 1.8 copy-start.1
Sparse Core Ops, SparseCore 0:
  263.4 54.1 reduce-scatter.1
